TPU v7x, 32 devices: a whole 2x2x4 slice. The times are simulated.
32 devices in a mesh: team: 2 (over x), blk: 4 (over z), head: 4 (over y, core).
Axes of the slice: x: 2, y: 2, z: 4, core: 2. Of those that a mesh axis runs over, the one named last changes fastest.
Arguments:
- queries: bfloat16 [1024, 8, 8, 128], P('blk', 'head', 'team'), may hold values from -40 to 40
- features: bfloat16 [1024, 8192], P('blk', ('team', 'head')), may hold values from -6 to 6
- adapter_down: bfloat16 [4, 8192, 64], P(None, ('team', 'head')), may hold values from -0.0625 to 0.0625
- adapter_key_up: bfloat16 [4, 64, 8, 128], P(None, None, 'head'), may hold values from -0.75 to 0.75
- adapter_value_up: bfloat16 [4, 64, 8, 128], P(None, None, 'head'), may hold values from -0.75 to 0.75
- base_key: bfloat16 [1024, 8, 128], P('blk', 'head'), may hold values from -6 to 6
- base_value: bfloat16 [1024, 8, 128], P('blk', 'head'), may hold values from -24 to 24
- prefix_key: bfloat16 [2048, 8, 128], P('blk', 'head'), may hold values from -7 to 7
- prefix_value: bfloat16 [2048, 8, 128], P('blk', 'head'), may hold values from -24 to 24
- adapter_ids: int32 [4], replicated, may hold values from 0 to 3
- block_order: int32 [4], replicated, may hold values from 0 to 15
Outputs:
- attended: bfloat16 [1024, 8, 8, 128], P('blk', 'head', 'team')
All inputs are finite; a program needn't handle non-finite values.
Results may differ from a plain program's by a relative error of at most 0.011.
Values may be sent and summed in bfloat16 or wider, within the bound.
No kernel may reach another device: no remote copies, remote signals or barrier semaphores. Data moves between devices by JAX's collectives and lax.ppermute only.
A program may use at most 64 MiB of HBM per device.

v0:
```python
import math
import jax
import jax.numpy as jnp
from jax import lax
from jax.sharding import PartitionSpec as P

NEG_FILL = -1e30


def block_length(row_count):
    for candidate in range(min(row_count, 1024), 0, -1):
        if row_count % candidate == 0:
            return candidate
    return row_count


def key_positions(row_count, shard_rows, prefix_dev, query_dev, block_order, block_count):
    row_index = jnp.arange(row_count, dtype=jnp.int32)
    holder = row_index // shard_rows
    within = row_index - holder * shard_rows
    block_ids = jnp.arange(block_count, dtype=jnp.int32)
    holder_order = jnp.sum(
        jnp.where(holder[:, None] == block_ids[None, :], block_order[None, :], 0), axis=1
    )
    later = prefix_dev * block_count + holder_order * query_dev + within - prefix_dev
    return jnp.where(within < prefix_dev, holder * prefix_dev + within, later)


def attend(running, query_rows, query_pos, key_rows, value_rows, key_pos):
    row_count = key_rows.shape[0]
    block_rows = block_length(row_count)
    key_blocks = row_count // block_rows
    kv_heads = key_rows.shape[1]
    head_dim = key_rows.shape[2]
    score_scale = 1.0 / math.sqrt(head_dim)
    latest = jnp.max(query_pos)
    key_split = key_rows.reshape((key_blocks, block_rows, kv_heads, head_dim))
    value_split = value_rows.reshape((key_blocks, block_rows, kv_heads, head_dim))
    pos_split = key_pos.reshape((key_blocks, block_rows))

    def advance(carried, block_data):
        block_keys, block_values, block_pos = block_data

        def compute(previous):
            row_max, row_sum, weighted = previous
            scores = (
                jnp.einsum(
                    "tkgd,skd->kgts", query_rows, block_keys, preferred_element_type=jnp.float32
                )
                * score_scale
            )
            visible = block_pos[None, None, None, :] <= query_pos[None, None, :, None]
            scores = jnp.where(visible, scores, NEG_FILL)
            new_max = jnp.maximum(row_max, jnp.max(scores, axis=-1))
            weights = jnp.where(visible, jnp.exp(scores - new_max[..., None]), 0.0)
            factor = jnp.exp(row_max - new_max)
            row_sum = row_sum * factor + jnp.sum(weights, axis=-1)
            product = jnp.einsum(
                "kgts,skd->kgtd",
                weights.astype(jnp.bfloat16),
                block_values,
                preferred_element_type=jnp.float32,
            )
            weighted = weighted * factor[..., None] + product
            return (new_max, row_sum, weighted)

        return (lax.cond(jnp.min(block_pos) > latest, lambda kept: kept, compute, carried), None)

    result, _ = lax.scan(advance, running, (key_split, value_split, pos_split))
    return result


def on_device(
    queries,
    features,
    adapter_down,
    adapter_key_up,
    adapter_value_up,
    base_key,
    base_value,
    prefix_key,
    prefix_value,
    adapter_ids,
    block_order,
):
    block_count = lax.axis_size("blk")
    my_block = lax.axis_index("blk")
    query_dev = queries.shape[0]
    kv_heads = queries.shape[1]
    group_dev = queries.shape[2]
    head_dim = queries.shape[3]
    prefix_dev = prefix_key.shape[0]
    rank_width = adapter_down.shape[2]
    shard_rows = prefix_dev + query_dev
    chosen = adapter_ids[my_block]
    down_rows = lax.dynamic_index_in_dim(adapter_down, chosen, 0, keepdims=False)
    partial_latent = jnp.dot(features, down_rows, preferred_element_type=jnp.float32)
    latent = lax.psum(partial_latent, ("team", "head")).astype(jnp.bfloat16)

    def expand(up_table, base_rows):
        up_rows = lax.dynamic_index_in_dim(up_table, chosen, 0, keepdims=False).reshape(
            rank_width, kv_heads * head_dim
        )
        delta = jnp.dot(latent, up_rows, preferred_element_type=jnp.float32).reshape(
            query_dev, kv_heads, head_dim
        )
        return (base_rows.astype(jnp.float32) + delta).astype(jnp.bfloat16)

    key_rows = jnp.concatenate([prefix_key, expand(adapter_key_up, base_key)], axis=0)
    value_rows = jnp.concatenate([prefix_value, expand(adapter_value_up, base_value)], axis=0)
    prefix_total = prefix_dev * block_count
    offsets = jnp.arange(query_dev, dtype=jnp.int32)
    query_pos = prefix_total + block_order[my_block] * query_dev + offsets
    initial = (
        jnp.full((kv_heads, group_dev, query_dev), NEG_FILL, jnp.float32),
        jnp.zeros((kv_heads, group_dev, query_dev), jnp.float32),
        jnp.zeros((kv_heads, group_dev, query_dev, head_dim), jnp.float32),
    )
    key_piece = lax.all_gather(key_rows, "blk", axis=0, tiled=True)
    value_piece = lax.all_gather(value_rows, "blk", axis=0, tiled=True)
    piece_pos = key_positions(
        key_piece.shape[0], shard_rows, prefix_dev, query_dev, block_order, block_count
    )
    row_max, row_sum, weighted = attend(
        initial, queries, query_pos, key_piece, value_piece, piece_pos
    )
    result = weighted / row_sum[..., None]
    return result.transpose(2, 0, 1, 3).astype(jnp.bfloat16)


def solution(mesh):
    placed = (
        P("blk", "head", "team", None),
        P("blk", ("team", "head")),
        P(None, ("team", "head"), None),
        P(None, None, "head", None),
        P(None, None, "head", None),
        P("blk", "head", None),
        P("blk", "head", None),
        P("blk", "head", None),
        P("blk", "head", None),
        P(),
        P(),
    )
    return jax.shard_map(
        on_device,
        mesh=mesh,
        in_specs=placed,
        out_specs=P("blk", "head", "team", None),
        check_vma=False,
    )
```

profile of v0, /device:TPU:0, one launch (start us, length us, event | category | flops | bytes accessed | tf_op | source)
XLA Modules:
  0.0 160.4 jit_solution(10820601032562232662)
XLA Ops:
  6.5 1.3 dynamic_slice.39
  9.8 1.2 convolution_bitcast_fusion
  11.0 26.0 %psum.7 = bf16[256,64]{0,1:T(8,128)(2,1)S(1)} all-reduce(f32[256,64]{0,1:T(8,128)S(1)} %convolution_bitcast_fusion), channel_id=1, replica_groups=mesh['team'=2,'blk'=4,'head'=4] {'team','head'}, use_global_device_ids=true, to_apply=%region_0.1 | all-reduce | flops 16384 | bytes 98304 | tf_op jit(solution)/shard_map/psum | solution.py:98
  37.0 1.0 copy.35
  38.0 0.8 constant_dynamic-slice_fusion.1
  38.8 1.1 fusion.21
  39.9 0.8 pad_maximum_fusion
  40.7 0.0 all-gather.3.cloned.1.call-update
  40.7 0.0 all-gather.5.cloned.1.call-start
  40.8 1.0 copy.38
  41.8 1.1 fusion.22
  42.9 0.8 pad_maximum_fusion.1
  43.6 0.0 all-gather.5.cloned.1.call-update
  43.7 1.2 dynamic_slice.38
  45.5 0.6 add_reduce_fusion
  46.1 1.1 copy.40
  47.2 0.8 select_reduce_fusion
  48.1 29.3 %all-gather.3.cloned.1.call-done = bf16[3072,2,128]{2,0,1:T(8,128)(2,1)} async-done(((bf16[768,2,128]{2,0,1:T(8,128)(2,1)}), bf16[3072,2,128]{2,0,1:T(8,128)(2,1)}) %all-gather.3.cloned.1.call-update) | async-done | bytes 1572880 | tf_op jit(solution)/shard_map/all_gather | solution.py:119
  77.4 1.5 copy.39
  78.9 36.0 %all-gather.5.cloned.1.call-done = bf16[3072,2,128]{2,0,1:T(8,128)(2,1)} async-done(((bf16[768,2,128]{2,0,1:T(8,128)(2,1)}), bf16[3072,2,128]{2,0,1:T(8,128)(2,1)}) %all-gather.5.cloned.1.call-update) | async-done | bytes 1572880 | tf_op jit(solution)/shard_map/all_gather | solution.py:120
  114.9 2.7 %copy.41 = bf16[3,1024,2,128]{3,1,2,0:T(8,128)(2,1)} copy(bf16[3,1024,2,128]{3,1,0,2:T(8,128)(2,1)} %bitcast.83) | data formatting | bytes 3145728
  117.6 1.0 broadcast_in_dim.56
  118.6 31.8 %while.15 = (s32[]{:T(128)}, f32[2,4,256]{2,1,0:T(4,128)S(1)}, f32[2,4,256]{2,1,0:T(4,128)S(1)}, f32[2,4,256,128]{3,2,1,0:T(8,128)}, s32[3,1024]{1,0:T(4,128)S(1...) while((s32[]{:T(128)}, f32[2,4,256]{2,1,0:T(4,128)S(1)}, ...), condition=%wide.region_9.10_spmd.clone, body=%wide.region_3.9_spmd.clone.sunk | while | flops 1101796608 | bytes 38421312 | solution.py:69
  118.6 0.6 fusion.45
  120.5 8.7 %conditional.3 = (f32[2,4,256]{2,1,0:T(4,128)S(1)}, f32[2,4,256]{2,1,0:T(4,128)S(1)}, f32[2,4,256,128]{3,2,1,0:T(8,128)}) conditional(s32[]{:T(128)} %convert_element_type.57, (s32[1,1024]{1,0:T(1,128)S(1)}, s32[]{:T(128)}, bf16[3,1024,2,128]{3,1,2,0:T(8,128)(2,1)S(1)}, s32[]{:T(128)}, bf16[256,2,4,128]{3,0,2,1:T(8,128)(2,1)S(1)}, ...), branch_computations={%region_5.7_spmd, %region_8.8_spmd} | conditional | flops 1101795584 | bytes 38395480 | solution.py:67
  120.5 0.2 broadcast_compare_fusion
  120.7 0.0 copy-start.1
  120.7 1.4 fusion.2
  122.2 2.0 %fusion.4 = f32[2,4,256]{2,1,0:T(4,128)S(1)} fusion(f32[2,1024,256,4]{2,1,3,0:T(8,128)S(1)} %get-tuple-element.228, f32[2,4,256]{2,1,0:T(4,128)S(1)} %max.4, pred[256,1024]{0,1:T(8,128)(4,1)S(1)} %broadcast_compare_fusion), kind=kLoop, calls=%fused_computation.5 | loop fusion | flops 10483712 | bytes 8667136 | tf_op jit(solution)/shard_map/while/body/eval_jaxpr/cond/branch_0_fun/reduce_sum | solution.py:57
  124.2 4.0 %fusion.8 = f32[2,4,256,128]{3,2,1,0:T(8,128)S(1)} fusion(f32[2,1024,256,4]{2,1,3,0:T(8,128)S(1)} %get-tuple-element.228, f32[2,4,256]{2,1,0:T(4,128)S(1)} %max.4, pred[256,1024]{0,1:T(8,128)(4,1)S(1)} %broadcast_compare_fusion, f32[2,4,256,128]{3,2,1,0:T(8,128)S(1)} %copy-done.1, bf16[3,1024,2,128]{3,1,2,0:T(8,128)(2,1)} %get-tuple-element.125, ...), kind=kOutput, calls=%fused_computation.8 | convolution fusion | flops 547880960 | bytes 11289088 | tf_op jit(solution)/shard_map/while/body/eval_jaxpr/cond/branch_0_fun/kgts,skd->kgtd/dot_general | solution.py:58
  128.3 1.0 copy-done.2
  129.2 0.6 fusion.45
  131.1 8.7 %conditional.3 = (f32[2,4,256]{2,1,0:T(4,128)S(1)}, f32[2,4,256]{2,1,0:T(4,128)S(1)}, f32[2,4,256,128]{3,2,1,0:T(8,128)}) conditional(s32[]{:T(128)} %convert_element_type.57, (s32[1,1024]{1,0:T(1,128)S(1)}, s32[]{:T(128)}, bf16[3,1024,2,128]{3,1,2,0:T(8,128)(2,1)S(1)}, s32[]{:T(128)}, bf16[256,2,4,128]{3,0,2,1:T(8,128)(2,1)S(1)}, ...), branch_computations={%region_5.7_spmd, %region_8.8_spmd} | conditional | flops 1101795584 | bytes 38395480 | solution.py:67
  131.1 0.2 broadcast_compare_fusion
  131.3 0.0 copy-start.1
  131.3 1.4 fusion.2
  132.8 2.0 %fusion.4 = f32[2,4,256]{2,1,0:T(4,128)S(1)} fusion(f32[2,1024,256,4]{2,1,3,0:T(8,128)S(1)} %get-tuple-element.228, f32[2,4,256]{2,1,0:T(4,128)S(1)} %max.4, pred[256,1024]{0,1:T(8,128)(4,1)S(1)} %broadcast_compare_fusion), kind=kLoop, calls=%fused_computation.5 | loop fusion | flops 10483712 | bytes 8667136 | tf_op jit(solution)/shard_map/while/body/eval_jaxpr/cond/branch_0_fun/reduce_sum | solution.py:57
  134.8 4.0 %fusion.8 = f32[2,4,256,128]{3,2,1,0:T(8,128)S(1)} fusion(f32[2,1024,256,4]{2,1,3,0:T(8,128)S(1)} %get-tuple-element.228, f32[2,4,256]{2,1,0:T(4,128)S(1)} %max.4, pred[256,1024]{0,1:T(8,128)(4,1)S(1)} %broadcast_compare_fusion, f32[2,4,256,128]{3,2,1,0:T(8,128)S(1)} %copy-done.1, bf16[3,1024,2,128]{3,1,2,0:T(8,128)(2,1)} %get-tuple-element.125, ...), kind=kOutput, calls=%fused_computation.8 | convolution fusion | flops 547880960 | bytes 11289088 | tf_op jit(solution)/shard_map/while/body/eval_jaxpr/cond/branch_0_fun/kgts,skd->kgtd/dot_general | solution.py:58
  138.9 1.0 copy-done.2
  139.8 0.6 fusion.45
  141.7 8.7 %conditional.3 = (f32[2,4,256]{2,1,0:T(4,128)S(1)}, f32[2,4,256]{2,1,0:T(4,128)S(1)}, f32[2,4,256,128]{3,2,1,0:T(8,128)}) conditional(s32[]{:T(128)} %convert_element_type.57, (s32[1,1024]{1,0:T(1,128)S(1)}, s32[]{:T(128)}, bf16[3,1024,2,128]{3,1,2,0:T(8,128)(2,1)S(1)}, s32[]{:T(128)}, bf16[256,2,4,128]{3,0,2,1:T(8,128)(2,1)S(1)}, ...), branch_computations={%region_5.7_spmd, %region_8.8_spmd} | conditional | flops 1101795584 | bytes 38395480 | solution.py:67
  141.7 0.2 broadcast_compare_fusion
  141.9 1.4 fusion.2
  143.4 2.0 %fusion.4 = f32[2,4,256]{2,1,0:T(4,128)S(1)} fusion(f32[2,1024,256,4]{2,1,3,0:T(8,128)S(1)} %get-tuple-element.228, f32[2,4,256]{2,1,0:T(4,128)S(1)} %max.4, pred[256,1024]{0,1:T(8,128)(4,1)S(1)} %broadcast_compare_fusion), kind=kLoop, calls=%fused_computation.5 | loop fusion | flops 10483712 | bytes 8667136 | tf_op jit(solution)/shard_map/while/body/eval_jaxpr/cond/branch_0_fun/reduce_sum | solution.py:57
  145.4 4.0 %fusion.8 = f32[2,4,256,128]{3,2,1,0:T(8,128)S(1)} fusion(f32[2,1024,256,4]{2,1,3,0:T(8,128)S(1)} %get-tuple-element.228, f32[2,4,256]{2,1,0:T(4,128)S(1)} %max.4, pred[256,1024]{0,1:T(8,128)(4,1)S(1)} %broadcast_compare_fusion, f32[2,4,256,128]{3,2,1,0:T(8,128)S(1)} %copy-done.1, bf16[3,1024,2,128]{3,1,2,0:T(8,128)(2,1)} %get-tuple-element.125, ...), kind=kOutput, calls=%fused_computation.8 | convolution fusion | flops 547880960 | bytes 11289088 | tf_op jit(solution)/shard_map/while/body/eval_jaxpr/cond/branch_0_fun/kgts,skd->kgtd/dot_general | solution.py:58
  149.5 1.0 copy-done.2
  150.4 0.2 copy.42
  150.6 2.9 %fusion.24 = bf16[256,2,4,128]{3,2,1,0:T(4,128)(2,1)} fusion(f32[2,4,256]{1,0,2:T(2,128)S(1)} %copy.42, f32[2,4,256,128]{3,2,1,0:T(8,128)} %get-tuple-element.142), kind=kLoop, calls=%fused_computation.31 | loop fusion | flops 524288 | bytes 1581056 | tf_op jit(solution)/shard_map/convert_element_type | solution.py:128
  (31 shorter events, 0.2 us)
Async XLA Ops:
  6.5 3.2 %copy-start = (bf16[256,1024]{1,0:T(8,128)(2,1)S(1)}, bf16[256,1024]{1,0:T(8,128)(2,1)}, u32[]{:S(2)}) copy-start(bf16[256,1024]{1,0:T(8,128)(2,1)} %param.16) | copy-start | bytes 1572868
  6.5 70.8 %all-gather.3.cloned.1.call-start = ((), (), s32[]{:S(2)}) async-start(), calls=%async_computation | async-start | bytes 1966080 | tf_op jit(solution)/shard_map/all_gather | solution.py:119
  40.7 74.2 %all-gather.5.cloned.1.call-start = ((), (), s32[]{:S(2)}) async-start(), calls=%async_computation.1 | async-start | bytes 1966080 | tf_op jit(solution)/shard_map/all_gather | solution.py:120
  120.7 3.5 %copy-start.1 = (f32[2,4,256,128]{3,2,1,0:T(8,128)S(1)}, f32[2,4,256,128]{3,2,1,0:T(8,128)}, u32[]{:S(2)}) copy-start(f32[2,4,256,128]{3,2,1,0:T(8,128)} %get-tuple-element.124) | copy-start | bytes 3145732 | tf_op jit(solution)/shard_map/while/body/eval_jaxpr/cond
  128.3 1.0 copy-start.2
  131.3 3.5 %copy-start.1 = (f32[2,4,256,128]{3,2,1,0:T(8,128)S(1)}, f32[2,4,256,128]{3,2,1,0:T(8,128)}, u32[]{:S(2)}) copy-start(f32[2,4,256,128]{3,2,1,0:T(8,128)} %get-tuple-element.124) | copy-start | bytes 3145732 | tf_op jit(solution)/shard_map/while/body/eval_jaxpr/cond
  138.9 1.0 copy-start.2
  141.9 3.5 %copy-start.1 = (f32[2,4,256,128]{3,2,1,0:T(8,128)S(1)}, f32[2,4,256,128]{3,2,1,0:T(8,128)}, u32[]{:S(2)}) copy-start(f32[2,4,256,128]{3,2,1,0:T(8,128)} %get-tuple-element.124) | copy-start | bytes 3145732 | tf_op jit(solution)/shard_map/while/body/eval_jaxpr/cond
  149.5 1.0 copy-start.2
Sparse Core Ops, SparseCore 0:
  40.8 36.4 all-gather.2
  78.9 35.9 all-gather.4
where the time goes:
time: 161 us; the launch traced here: 160 us
  waiting for transfers between devices  65.4 us (41%)
  blocking collectives  26 us (16%)
  matrix products  19.7 us (12%)
  between operations  16 us (10%)
  local copies, waits for them, and re-layouts  14.8 us (9%)
  other arithmetic  14.6 us (9%)
  loops' own time  3.9 us (2%)
    all_gather x1, waiting for transfers between devices, on_device(): value_piece = lax.all_gather(value_rows, 'blk', axis=0, tiled=True)  36 us
    all_gather x1, waiting for transfers between devices, on_device(): key_piece = lax.all_gather(key_rows, 'blk', axis=0, tiled=True)  29.3 us
    psum x1, blocking collectives, on_device(): latent = lax.psum(partial_latent, ('team', 'head')).astype(jnp.bfloat16)  26 us
    dot_general x3, matrix products, compute(): jnp.einsum('kgts,skd->kgtd', weights.astype(jnp.bfloat16), block_values,...  12.1 us
    unnamed x7, local copies, waits for them, and re-layouts  7.28 us
    reduce_sum x3, other arithmetic, compute(): row_sum = row_sum * factor + jnp.sum(weights, axis=-1)  6.09 us
    dot_general x3, matrix products, compute(): jnp.einsum('tkgd,skd->kgts', query_rows, block_keys, preferred_element_ty...  4.2 us
    another operation x1, loops' own time, attend(): result, _ = lax.scan(advance, running, (key_split, value_split, pos_split))  3.67 us
  transfers between devices with their start and end apart: 2, of which 2 were waited for; matrix products, arithmetic and copies ran while one was open for 5% of the time, Pallas kernels for 0%

commit v1 on v0

--- a/solution.py
+++ b/solution.py
@@ -5,6 +5,17 @@
 from jax.sharding import PartitionSpec as P
 
 NEG_FILL = -1e30
+
+
+def around_the_ring(x, axis, along):
+    devices = lax.axis_size(axis)
+    right = [(i, (i + 1) % devices) for i in range(devices)]
+    parts = [x]
+    for far in range(1, devices):
+        parts = [lax.ppermute(parts[0], axis, right), *parts]
+    whole = jnp.concatenate(parts, axis=along)
+    places = (lax.axis_index(axis) + 1) * parts[-1].shape[along]
+    return jnp.roll(whole, places, axis=along)
 
 
 def block_length(row_count):
@@ -117,7 +128,7 @@
         jnp.zeros((kv_heads, group_dev, query_dev, head_dim), jnp.float32),
     )
     key_piece = lax.all_gather(key_rows, "blk", axis=0, tiled=True)
-    value_piece = lax.all_gather(value_rows, "blk", axis=0, tiled=True)
+    value_piece = around_the_ring(value_rows, "blk", 0)
     piece_pos = key_positions(
         key_piece.shape[0], shard_rows, prefix_dev, query_dev, block_order, block_count
     )

time: 161 us -> 144 us (0.89)
  the two profiles are of different devices: /device:TPU:0 before, /device:TPU:4 now
where the time goes in v1:
time: 144 us
  waiting for transfers between devices  54.6 us (38%)
  blocking collectives  21.9 us (15%)
  matrix products  19.7 us (14%)
  between operations  16.1 us (11%)
  other arithmetic  13.2 us (9%)
  local copies, waits for them, and re-layouts  12.6 us (9%)
  loops' own time  3.84 us (3%)
  starting transfers between devices  1.63 us (1%)
    ppermute x3, waiting for transfers between devices, around_the_ring(): parts = [lax.ppermute(parts[0], axis, right), *parts]  41 us
    psum x1, blocking collectives, on_device(): latent = lax.psum(partial_latent, ('team', 'head')).astype(jnp.bfloat16)  21.9 us
    all_gather x1, waiting for transfers between devices, on_device(): key_piece = lax.all_gather(key_rows, 'blk', axis=0, tiled=True)  13.6 us
    dot_general x3, matrix products, compute(): jnp.einsum('kgts,skd->kgtd', weights.astype(jnp.bfloat16), block_values,...  12.1 us
    reduce_sum x3, other arithmetic, compute(): row_sum = row_sum * factor + jnp.sum(weights, axis=-1)  6.09 us
    unnamed x22, local copies, waits for them, and re-layouts  5.3 us
    dot_general x3, matrix products, compute(): jnp.einsum('tkgd,skd->kgts', query_rows, block_keys, preferred_element_ty...  4.2 us
    another operation x1, loops' own time, attend(): result, _ = lax.scan(advance, running, (key_split, value_split, pos_split))  3.61 us
  transfers between devices with their start and end apart: 4, of which 4 were waited for; matrix products, arithmetic and copies ran while one was open for 5% of the time, Pallas kernels for 0%

profile of v1, /device:TPU:4, one launch (start us, length us, event | category | flops | bytes accessed | tf_op | source)
XLA Modules:
  0.0 143.7 jit_solution(11553107753300940171)
XLA Ops:
  6.6 1.3 dynamic_slice.43
  9.8 1.2 convolution_bitcast_fusion
  11.0 21.9 %psum.7 = bf16[256,64]{0,1:T(8,128)(2,1)S(1)} all-reduce(f32[256,64]{0,1:T(8,128)S(1)} %convolution_bitcast_fusion), channel_id=1, replica_groups=mesh['team'=2,'blk'=4,'head'=4] {'team','head'}, use_global_device_ids=true, to_apply=%region_0.1 | all-reduce | flops 16384 | bytes 98304 | tf_op jit(solution)/shard_map/psum | solution.py:109
  32.9 1.0 copy.42
  33.9 0.8 constant_dynamic-slice_fusion.2
  34.7 1.1 fusion.22
  35.9 1.6 %collective-permute-start = (bf16[768,2,128]{2,0,1:T(8,128)(2,1)S(1)}, bf16[768,2,128]{2,0,1:T(8,128)(2,1)S(1)}, u32[]{:S(2)}, u32[]{:S(2)}) collective-permute-start(bf16[768,2,128]{2,0,1:T(8,128)(2,1)S(1)} %pad_maximum_fusion.1), channel_id=1, source_target_pairs={{0,4},{4,8},{8,12},{12,0},{1,5},{5,9},{9,13},{13,1},{2,6},{6,10},{... | collective-permute-start | bytes 1179656 | tf_op jit(solution)/shard_map/ppermute | solution.py:15
  37.5 12.0 %collective-permute-done = bf16[768,2,128]{2,0,1:T(8,128)(2,1)S(1)} collective-permute-done((bf16[768,2,128]{2,0,1:T(8,128)(2,1)S(1)}, bf16[768,2,128]{2,0,1:T(8,128)(2,1)S(1)}, u32[]{:S(2)}, u32[]{:S(2)}) %collective-permute-start) | collective-permute-done | bytes 393248 | tf_op jit(solution)/shard_map/ppermute | solution.py:15
  49.6 1.1 fusion.21
  50.7 1.0 copy.39
  51.7 0.8 pad_maximum_fusion
  52.5 0.6 dynamic_slice.42
  53.7 0.6 add_reduce_fusion
  54.3 0.1 copy.46
  54.4 0.1 select_reduce_fusion
  54.5 7.8 %collective-permute-done.1 = bf16[768,2,128]{2,0,1:T(8,128)(2,1)S(1)} collective-permute-done((bf16[768,2,128]{2,0,1:T(8,128)(2,1)S(1)}, bf16[768,2,128]{2,0,1:T(8,128)(2,1)S(1)}, u32[]{:S(2)}, u32[]{:S(2)}) %collective-permute-start.1) | collective-permute-done | bytes 393248 | tf_op jit(solution)/shard_map/ppermute | solution.py:15
  62.4 21.2 %collective-permute-done.2 = bf16[768,2,128]{2,0,1:T(8,128)(2,1)S(1)} collective-permute-done((bf16[768,2,128]{2,0,1:T(8,128)(2,1)S(1)}, bf16[768,2,128]{2,0,1:T(8,128)(2,1)S(1)}, u32[]{:S(2)}, u32[]{:S(2)}) %collective-permute-start.2) | collective-permute-done | bytes 393248 | tf_op jit(solution)/shard_map/ppermute | solution.py:15
  83.8 0.1 constant_dynamic-update-slice_fusion.6
  84.0 0.1 constant_dynamic-update-slice_fusion.1
  84.1 0.4 constant_dynamic-slice_fusion.1
  84.6 1.3 copy.47
  85.8 13.6 %all-gather.2.cloned.1.call-done = bf16[3072,2,128]{2,0,1:T(8,128)(2,1)} async-done(((bf16[768,2,128]{2,0,1:T(8,128)(2,1)}), bf16[3072,2,128]{2,0,1:T(8,128)(2,1)}) %all-gather.2.cloned.1.call-update) | async-done | bytes 1572880 | tf_op jit(solution)/shard_map/all_gather | solution.py:130
  99.4 1.5 %copy.45 = bf16[3,1024,2,128]{3,1,2,0:T(8,128)(2,1)S(1)} copy(bf16[3,1024,2,128]{3,1,0,2:T(8,128)(2,1)} %bitcast.83) | data formatting | bytes 3145728
  100.9 1.1 broadcast_in_dim.56
  102.0 31.8 %while.15 = (s32[]{:T(128)}, f32[2,4,256]{2,1,0:T(4,128)S(1)}, f32[2,4,256]{2,1,0:T(4,128)S(1)}, f32[2,4,256,128]{3,2,1,0:T(8,128)}, s32[3,1024]{1,0:T(4,128)S(1...) while((s32[]{:T(128)}, f32[2,4,256]{2,1,0:T(4,128)S(1)}, ...), condition=%wide.region_9.10_spmd.clone, body=%wide.region_3.9_spmd.clone.sunk | while | flops 1101796608 | bytes 38421312 | solution.py:80
  102.0 0.6 fusion.45
  103.8 8.7 %conditional.3 = (f32[2,4,256]{2,1,0:T(4,128)S(1)}, f32[2,4,256]{2,1,0:T(4,128)S(1)}, f32[2,4,256,128]{3,2,1,0:T(8,128)}) conditional(s32[]{:T(128)} %convert_element_type.57, (s32[1,1024]{1,0:T(1,128)S(1)}, s32[]{:T(128)}, bf16[3,1024,2,128]{3,1,2,0:T(8,128)(2,1)S(1)}, s32[]{:T(128)}, bf16[256,2,4,128]{3,0,2,1:T(8,128)(2,1)S(1)}, ...), branch_computations={%region_5.7_spmd, %region_8.8_spmd} | conditional | flops 1101795584 | bytes 38395480 | solution.py:78
  103.8 0.2 broadcast_compare_fusion
  104.1 1.4 fusion.2
  105.5 2.0 %fusion.4 = f32[2,4,256]{2,1,0:T(4,128)S(1)} fusion(f32[2,1024,256,4]{2,1,3,0:T(8,128)S(1)} %get-tuple-element.228, f32[2,4,256]{2,1,0:T(4,128)S(1)} %max.4, pred[256,1024]{0,1:T(8,128)(4,1)S(1)} %broadcast_compare_fusion), kind=kLoop, calls=%fused_computation.5 | loop fusion | flops 10483712 | bytes 8667136 | tf_op jit(solution)/shard_map/while/body/eval_jaxpr/cond/branch_0_fun/reduce_sum | solution.py:68
  107.5 4.0 %fusion.8 = f32[2,4,256,128]{3,2,1,0:T(8,128)S(1)} fusion(f32[2,1024,256,4]{2,1,3,0:T(8,128)S(1)} %get-tuple-element.228, f32[2,4,256]{2,1,0:T(4,128)S(1)} %max.4, pred[256,1024]{0,1:T(8,128)(4,1)S(1)} %broadcast_compare_fusion, f32[2,4,256,128]{3,2,1,0:T(8,128)S(1)} %copy-done.1, bf16[3,1024,2,128]{3,1,2,0:T(8,128)(2,1)} %get-tuple-element.125, ...), kind=kOutput, calls=%fused_computation.8 | convolution fusion | flops 547880960 | bytes 11289088 | tf_op jit(solution)/shard_map/while/body/eval_jaxpr/cond/branch_0_fun/kgts,skd->kgtd/dot_general | solution.py:69
  111.6 1.0 copy-done.2
  112.5 0.6 fusion.45
  114.4 8.7 %conditional.3 = (f32[2,4,256]{2,1,0:T(4,128)S(1)}, f32[2,4,256]{2,1,0:T(4,128)S(1)}, f32[2,4,256,128]{3,2,1,0:T(8,128)}) conditional(s32[]{:T(128)} %convert_element_type.57, (s32[1,1024]{1,0:T(1,128)S(1)}, s32[]{:T(128)}, bf16[3,1024,2,128]{3,1,2,0:T(8,128)(2,1)S(1)}, s32[]{:T(128)}, bf16[256,2,4,128]{3,0,2,1:T(8,128)(2,1)S(1)}, ...), branch_computations={%region_5.7_spmd, %region_8.8_spmd} | conditional | flops 1101795584 | bytes 38395480 | solution.py:78
  114.4 0.2 broadcast_compare_fusion
  114.6 1.4 fusion.2
  116.1 2.0 %fusion.4 = f32[2,4,256]{2,1,0:T(4,128)S(1)} fusion(f32[2,1024,256,4]{2,1,3,0:T(8,128)S(1)} %get-tuple-element.228, f32[2,4,256]{2,1,0:T(4,128)S(1)} %max.4, pred[256,1024]{0,1:T(8,128)(4,1)S(1)} %broadcast_compare_fusion), kind=kLoop, calls=%fused_computation.5 | loop fusion | flops 10483712 | bytes 8667136 | tf_op jit(solution)/shard_map/while/body/eval_jaxpr/cond/branch_0_fun/reduce_sum | solution.py:68
  118.1 4.0 %fusion.8 = f32[2,4,256,128]{3,2,1,0:T(8,128)S(1)} fusion(f32[2,1024,256,4]{2,1,3,0:T(8,128)S(1)} %get-tuple-element.228, f32[2,4,256]{2,1,0:T(4,128)S(1)} %max.4, pred[256,1024]{0,1:T(8,128)(4,1)S(1)} %broadcast_compare_fusion, f32[2,4,256,128]{3,2,1,0:T(8,128)S(1)} %copy-done.1, bf16[3,1024,2,128]{3,1,2,0:T(8,128)(2,1)} %get-tuple-element.125, ...), kind=kOutput, calls=%fused_computation.8 | convolution fusion | flops 547880960 | bytes 11289088 | tf_op jit(solution)/shard_map/while/body/eval_jaxpr/cond/branch_0_fun/kgts,skd->kgtd/dot_general | solution.py:69
  122.2 1.0 copy-done.2
  123.1 0.6 fusion.45
  125.0 8.7 %conditional.3 = (f32[2,4,256]{2,1,0:T(4,128)S(1)}, f32[2,4,256]{2,1,0:T(4,128)S(1)}, f32[2,4,256,128]{3,2,1,0:T(8,128)}) conditional(s32[]{:T(128)} %convert_element_type.57, (s32[1,1024]{1,0:T(1,128)S(1)}, s32[]{:T(128)}, bf16[3,1024,2,128]{3,1,2,0:T(8,128)(2,1)S(1)}, s32[]{:T(128)}, bf16[256,2,4,128]{3,0,2,1:T(8,128)(2,1)S(1)}, ...), branch_computations={%region_5.7_spmd, %region_8.8_spmd} | conditional | flops 1101795584 | bytes 38395480 | solution.py:78
  125.0 0.2 broadcast_compare_fusion
  125.2 1.4 fusion.2
  126.7 2.0 %fusion.4 = f32[2,4,256]{2,1,0:T(4,128)S(1)} fusion(f32[2,1024,256,4]{2,1,3,0:T(8,128)S(1)} %get-tuple-element.228, f32[2,4,256]{2,1,0:T(4,128)S(1)} %max.4, pred[256,1024]{0,1:T(8,128)(4,1)S(1)} %broadcast_compare_fusion), kind=kLoop, calls=%fused_computation.5 | loop fusion | flops 10483712 | bytes 8667136 | tf_op jit(solution)/shard_map/while/body/eval_jaxpr/cond/branch_0_fun/reduce_sum | solution.py:68
  128.7 4.0 %fusion.8 = f32[2,4,256,128]{3,2,1,0:T(8,128)S(1)} fusion(f32[2,1024,256,4]{2,1,3,0:T(8,128)S(1)} %get-tuple-element.228, f32[2,4,256]{2,1,0:T(4,128)S(1)} %max.4, pred[256,1024]{0,1:T(8,128)(4,1)S(1)} %broadcast_compare_fusion, f32[2,4,256,128]{3,2,1,0:T(8,128)S(1)} %copy-done.1, bf16[3,1024,2,128]{3,1,2,0:T(8,128)(2,1)} %get-tuple-element.125, ...), kind=kOutput, calls=%fused_computation.8 | convolution fusion | flops 547880960 | bytes 11289088 | tf_op jit(solution)/shard_map/while/body/eval_jaxpr/cond/branch_0_fun/kgts,skd->kgtd/dot_general | solution.py:69
  132.8 1.0 copy-done.2
  133.7 0.2 copy.48
  133.9 2.9 %fusion.24 = bf16[256,2,4,128]{3,2,1,0:T(4,128)(2,1)} fusion(f32[2,4,256]{1,0,2:T(2,128)S(1)} %copy.48, f32[2,4,256,128]{3,2,1,0:T(8,128)} %get-tuple-element.142), kind=kLoop, calls=%fused_computation.31 | loop fusion | flops 524288 | bytes 1581056 | tf_op jit(solution)/shard_map/convert_element_type | solution.py:139
  (51 shorter events, 0.6 us)
Async XLA Ops:
  6.5 3.3 %copy-start = (bf16[256,1024]{1,0:T(8,128)(2,1)S(1)}, bf16[256,1024]{1,0:T(8,128)(2,1)}, u32[]{:S(2)}) copy-start(bf16[256,1024]{1,0:T(8,128)(2,1)} %param.16) | copy-start | bytes 1572868
  6.5 46.0 %copy-start.5 = (s32[4]{0:T(128)S(1)}, s32[4]{0:T(128)}, u32[]{:S(2)}) copy-start(s32[4]{0:T(128)} %param.25) | copy-start | bytes 52
  6.5 47.7 %copy-start.4 = (bf16[256,2,4,128]{3,2,1,0:T(4,128)(2,1)S(1)}, bf16[256,2,4,128]{3,2,1,0:T(4,128)(2,1)}, u32[]{:S(2)}) copy-start(bf16[256,2,4,128]{3,2,1,0:T(4,128)(2,1)} %param.15) | copy-start | bytes 1572868
  6.5 92.9 %all-gather.2.cloned.1.call-start = ((), (), s32[]{:S(2)}) async-start(), calls=%async_computation | async-start | bytes 1966080 | tf_op jit(solution)/shard_map/all_gather | solution.py:130
  35.9 47.9 %copy-start.3 = (bf16[512,2,128]{2,1,0:T(2,128)(2,1)S(1)}, bf16[512,2,128]{2,1,0:T(2,128)(2,1)}, u32[]{:S(2)}) copy-start(bf16[512,2,128]{2,1,0:T(2,128)(2,1)} %param.23) | copy-start | bytes 786436
  35.9 13.6 %collective-permute-start = (bf16[768,2,128]{2,0,1:T(8,128)(2,1)S(1)}, bf16[768,2,128]{2,0,1:T(8,128)(2,1)S(1)}, u32[]{:S(2)}, u32[]{:S(2)}) collective-permute-start(bf16[768,2,128]{2,0,1:T(8,128)(2,1)S(1)} %pad_maximum_fusion.1), channel_id=1, source_target_pairs={{0,4},{4,8},{8,12},{12,0},{1,5},{5,9},{9,13},{13,1},{2,6},{6,10},{... | collective-permute-start | bytes 1179656 | tf_op jit(solution)/shard_map/ppermute | solution.py:15
  49.6 12.7 %collective-permute-start.1 = (bf16[768,2,128]{2,0,1:T(8,128)(2,1)S(1)}, bf16[768,2,128]{2,0,1:T(8,128)(2,1)S(1)}, u32[]{:S(2)}, u32[]{:S(2)}) collective-permute-start(bf16[768,2,128]{2,0,1:T(8,128)(2,1)S(1)} %collective-permute-done), channel_id=1, source_target_pairs={{0,4},{4,8},{8,12},{12,0},{1,5},{5,9},{9,13},{13,1},{2,6},{6,10},{... | collective-permute-start | bytes 1179656 | tf_op jit(solution)/shard_map/ppermute | solution.py:15
  62.3 21.3 %collective-permute-start.2 = (bf16[768,2,128]{2,0,1:T(8,128)(2,1)S(1)}, bf16[768,2,128]{2,0,1:T(8,128)(2,1)S(1)}, u32[]{:S(2)}, u32[]{:S(2)}) collective-permute-start(bf16[768,2,128]{2,0,1:T(8,128)(2,1)S(1)} %collective-permute-done.1), channel_id=1, source_target_pairs={{0,4},{4,8},{8,12},{12,0},{1,5},{5,9},{9,13},{13,1},{2,6},{6,10},{... | collective-permute-start | bytes 1179656 | tf_op jit(solution)/shard_map/ppermute | solution.py:15
  105.5 2.1 %copy-start.1 = (f32[2,4,256,128]{3,2,1,0:T(8,128)S(1)}, f32[2,4,256,128]{3,2,1,0:T(8,128)}, u32[]{:S(2)}) copy-start(f32[2,4,256,128]{3,2,1,0:T(8,128)} %get-tuple-element.124) | copy-start | bytes 3145732 | tf_op jit(solution)/shard_map/while/body/eval_jaxpr/cond
  111.6 1.0 copy-start.2
  116.1 2.1 %copy-start.1 = (f32[2,4,256,128]{3,2,1,0:T(8,128)S(1)}, f32[2,4,256,128]{3,2,1,0:T(8,128)}, u32[]{:S(2)}) copy-start(f32[2,4,256,128]{3,2,1,0:T(8,128)} %get-tuple-element.124) | copy-start | bytes 3145732 | tf_op jit(solution)/shard_map/while/body/eval_jaxpr/cond
  122.2 1.0 copy-start.2
  126.6 2.1 %copy-start.1 = (f32[2,4,256,128]{3,2,1,0:T(8,128)S(1)}, f32[2,4,256,128]{3,2,1,0:T(8,128)}, u32[]{:S(2)}) copy-start(f32[2,4,256,128]{3,2,1,0:T(8,128)} %get-tuple-element.124) | copy-start | bytes 3145732 | tf_op jit(solution)/shard_map/while/body/eval_jaxpr/cond
  132.8 1.0 copy-start.2
Sparse Core Ops, SparseCore 0:
  52.6 46.7 all-gather.1
